TPU v7x, 512 devices: a whole 4x8x8 slice. The times are simulated.
512 devices in a mesh: au: 32 (over z, y_lo), ia: 16 (over x, y_hi, core).
Axes of the slice: x: 4, y: 8 (y_hi: 2, y_lo: 4; y = y_hi * 4 + y_lo), z: 8, core: 2. Of those that a mesh axis runs over, the one named last changes fastest.
Arguments:
- user_emb: bfloat16 [32, 2048, 256], P('au', 'ia'), may hold values from -6 to 6
- item_emb: bfloat16 [16, 1024, 256], P('ia', 'au'), may hold values from -6 to 6
- weight: bfloat16 [256, 256], replicated, may hold values from -0.375 to 0.375
- grad_user: bfloat16 [32, 2048, 256], P('au', 'ia'), may hold values from -6 to 6
- grad_item: bfloat16 [16, 1024, 256], P('ia', 'au'), may hold values from -6 to 6
- tile_values: bfloat16 [32, 2048, 128, 128], P('au', 'ia'), may hold values from 0 to 1
- tile_rows: int32 [32, 2048], P('au', 'ia'), may hold values from 0 to 15
- tile_cols: int32 [32, 2048], P('au', 'ia'), may hold values from 0 to 7
- tile_norm: int32 [32, 2048], P('au', 'ia'), may hold values from 32 to 128
- tile_count: int32 [32, 16], P('au', 'ia'), may hold values from 64 to 128, as said below
Outputs:
- grad_user_emb: bfloat16 [32, 2048, 256], P('au', 'ia')
- grad_item_emb: bfloat16 [16, 1024, 256], P('ia', 'au')
- grad_weight: float32 [256, 256], replicated
Inputs may be any that keep to these rules, and one draw needn't show every extreme that they name: `tile_rows`: slots of one block pair may name the same tile position; their terms add. Slots at and after tile_count[a, b] are unused; some block pair has exactly 128 live slots in every draw.
All inputs are finite; a program needn't handle non-finite values.
Results may differ from a plain program's by a relative error of at most 0.025.
Values may be sent and summed in bfloat16 or wider, within the bound.
No kernel may reach another device: no remote copies, remote signals or barrier semaphores. Data moves between devices by JAX's collectives and lax.ppermute only.
A program may use at most 64 MiB of HBM per device.

v0:
```python
import math
import jax
import jax.numpy as jnp
from jax import lax
from jax.sharding import PartitionSpec as P

slot_group = 8


def from_everyone(value, axis):
    copies = jnp.broadcast_to(value, (lax.axis_size(axis), *value.shape))
    return lax.all_to_all(copies, axis, split_axis=0, concat_axis=0, tiled=True)


def in_order(pieces, dim):
    pieces = jnp.moveaxis(pieces, 0, dim)
    shape = pieces.shape
    return pieces.reshape(*shape[:dim], shape[dim] * shape[dim + 1], *shape[dim + 2 :])


def collect(value, axis, dim):
    pieces = from_everyone(value, axis)
    return in_order(pieces, dim)


def in_blocks(value, dim, peers):
    shape = value.shape
    pieces = value.reshape(*shape[:dim], peers, shape[dim] // peers, *shape[dim + 1 :])
    return jnp.moveaxis(pieces, dim, 0)


def summed_on_arrival(value, axis, dim):
    pieces = in_blocks(value, dim, lax.axis_size(axis))
    arrived = lax.all_to_all(pieces, axis, split_axis=0, concat_axis=0, tiled=True)
    return arrived.astype(jnp.float32).sum(axis=0)


def split_tiles(block, edge):
    return block.reshape(-1, edge, block.shape[-1])


def fetch_items(grad_item, edge):
    cotangent = collect(grad_item, "au", 1)
    return (split_tiles(cotangent[0], edge), None)


def fetch_users(grad_user, edge):
    cotangent = collect(grad_user, "ia", 1)
    return (split_tiles(cotangent[0], edge), None)


def sweep(
    tile_block,
    row_ids,
    col_ids,
    norm_ids,
    live_count,
    item_source,
    user_source,
    user_shape,
    item_shape,
):
    turn_count = (live_count + slot_group - 1) // slot_group
    placeholder = jnp.zeros((1,), jnp.float32)

    def one_turn(turn_index, totals):
        user_total, item_total = totals
        first_slot = turn_index * slot_group
        values = lax.dynamic_slice_in_dim(tile_block, first_slot, slot_group, 0)
        row_pick = lax.dynamic_slice_in_dim(row_ids, first_slot, slot_group, 0)
        col_pick = lax.dynamic_slice_in_dim(col_ids, first_slot, slot_group, 0)
        norm_pick = lax.dynamic_slice_in_dim(norm_ids, first_slot, slot_group, 0)
        live_mask = first_slot + jnp.arange(slot_group, dtype=jnp.int32) < live_count
        inverse = jnp.where(live_mask, 1.0 / norm_pick.astype(jnp.float32), 0.0)[:, None, None]
        if item_source is not None:
            forward = jnp.einsum(
                "gic,gcd->gid", values, item_source[col_pick], preferred_element_type=jnp.float32
            )
            user_total = user_total.at[row_pick].add(forward * inverse)
        if user_source is not None:
            backward = jnp.einsum(
                "gic,gid->gcd", values, user_source[row_pick], preferred_element_type=jnp.float32
            )
            item_total = item_total.at[col_pick].add(backward * inverse)
        return (user_total, item_total)

    start = (
        jnp.zeros(user_shape, jnp.float32) if item_source is not None else placeholder,
        jnp.zeros(item_shape, jnp.float32) if user_source is not None else placeholder,
    )
    return lax.fori_loop(0, turn_count, one_turn, start)


def reduce_users(user_total, width):
    return summed_on_arrival(user_total.reshape(-1, width).astype(jnp.bfloat16), "ia", 0)


def reduce_items(item_total, width):
    return summed_on_arrival(item_total.reshape(-1, width).astype(jnp.bfloat16), "au", 0)


def block_product(embedded, total):
    return jnp.einsum(
        "rd,re->de", embedded.astype(jnp.float32), total, precision=lax.Precision.HIGHEST
    )


def per_device(
    user_emb,
    item_emb,
    weight,
    grad_user,
    grad_item,
    tile_values,
    tile_rows,
    tile_cols,
    tile_norm,
    tile_count,
):
    width = weight.shape[0]
    edge = tile_values.shape[2]
    user_shape = (user_emb.shape[1] * lax.axis_size("ia") // edge, edge, width)
    item_shape = (item_emb.shape[1] * lax.axis_size("au") // edge, edge, width)
    tile_block = tile_values[0]
    row_ids = tile_rows[0]
    col_ids = tile_cols[0]
    norm_ids = tile_norm[0]
    live_count = tile_count[0, 0]
    item_source, item_rows = fetch_items(grad_item, edge)
    user_total, unused = sweep(
        tile_block,
        row_ids,
        col_ids,
        norm_ids,
        live_count,
        item_source,
        None,
        user_shape,
        item_shape,
    )
    q_user = reduce_users(user_total, width)
    user_source, user_rows = fetch_users(grad_user, edge)
    unused, item_total = sweep(
        tile_block,
        row_ids,
        col_ids,
        norm_ids,
        live_count,
        None,
        user_source,
        user_shape,
        item_shape,
    )
    q_item = reduce_items(item_total, width)
    weight_part = block_product(user_emb[0], q_user) + block_product(item_emb[0], q_item)
    user_count = user_emb.shape[1] * lax.axis_size("ia") * lax.axis_size("au")
    item_count = item_emb.shape[1] * lax.axis_size("au") * lax.axis_size("ia")
    grad_weight = lax.psum(weight_part, ("au", "ia")) / math.sqrt(user_count + item_count)
    grad_user_emb = jnp.einsum(
        "re,de->rd", q_user.astype(jnp.bfloat16), weight, preferred_element_type=jnp.float32
    ).astype(jnp.bfloat16)
    grad_item_emb = jnp.einsum(
        "re,de->rd", q_item.astype(jnp.bfloat16), weight, preferred_element_type=jnp.float32
    ).astype(jnp.bfloat16)
    return (grad_user_emb[None], grad_item_emb[None], grad_weight)


def solution(mesh):
    return jax.shard_map(
        per_device,
        mesh=mesh,
        in_specs=(
            P("au", "ia", None),
            P("ia", "au", None),
            P(),
            P("au", "ia", None),
            P("ia", "au", None),
            P("au", "ia", None, None),
            P("au", "ia"),
            P("au", "ia"),
            P("au", "ia"),
            P("au", "ia"),
        ),
        out_specs=(P("au", "ia", None), P("ia", "au", None), P()),
        check_vma=False,
    )
```

profile of v0, /device:TPU:23, one launch (start us, length us, event | category | flops | bytes accessed | tf_op | source)
XLA Modules:
  0.0 567.4 jit_solution(4700820097756876434)
XLA Ops:
  9.2 8.5 %all-to-all-start.2 = ((bf16[16,1,128,256]{3,2,1,0:T(8,128)(2,1)}), bf16[16,1,128,256]{3,2,1,0:T(8,128)(2,1)}, u32[]{:S(2)}, u32[]{:S(2)}) async-start(bf16[16,1,128,256]{3,2,1,0:T(8,128)(2,1)} %broadcast_in_dim.43), calls=%async_computation.2 | async-start | bytes 2097152 | tf_op jit(solution)/shard_map/all_to_all | solution.py:12
  18.4 6.4 %copy.16 = bf16[1,128,128,128]{2,3,1,0:T(8,128)(2,1)} copy(bf16[1,128,128,128]{3,2,1,0:T(8,128)(2,1)} %param.19) | data formatting | bytes 8388608 | tf_op args[5]
  24.8 21.8 %all-to-all-done.2 = bf16[16,1,128,256]{3,2,1,0:T(8,128)(2,1)} async-done(((bf16[16,1,128,256]{3,2,1,0:T(8,128)(2,1)}), bf16[16,1,128,256]{3,2,1,0:T(8,128)(2,1)}, u32[]{:S(2)}, u32[]{:S(2)}) %all-to-all-start.2) | async-done | bytes 1048608 | tf_op jit(solution)/shard_map/all_to_all | solution.py:12
  47.4 12.4 %all-to-all-start = ((bf16[32,1,32,256]{3,2,1,0:T(8,128)(2,1)}), bf16[32,1,32,256]{3,2,1,0:T(8,128)(2,1)S(1)}, u32[]{:S(2)}, u32[]{:S(2)}) async-start(bf16[32,1,32,256]{3,2,1,0:T(8,128)(2,1)} %broadcast_in_dim.40), calls=%async_computation | async-start | bytes 1048576 | tf_op jit(solution)/shard_map/all_to_all | solution.py:12
  59.9 68.0 %while.21 = (s32[]{:T(128)}, f32[8,128,256]{2,1,0:T(8,128)S(1)}, s32[]{:T(128)}, s32[128]{0:T(128)S(1)}, bf16[128,128,128]{1,2,0:T(8,128)(2,1)}, /*index=5*/s32[...) while((s32[]{:T(128)}, f32[8,128,256]{2,1,0:T(8,128)S(1)}, ...), condition=%wide.region_6.7_spmd, body=%wide.region_4.6_spmd.sunk | while | flops 67634272 | bytes 6033919 | solution.py:91
  128.8 24.3 %all-to-all-start.3 = ((bf16[32,32,256]{2,1,0:T(8,128)(2,1)}), bf16[32,32,256]{2,1,0:T(8,128)(2,1)S(1)}, u32[]{:S(2)}, u32[]{:S(2)}) async-start(bf16[32,32,256]{2,1,0:T(8,128)(2,1)} %bitcast.11), calls=%async_computation.3 | async-start | bytes 1048576 | tf_op jit(solution)/shard_map/all_to_all | solution.py:34
  154.7 77.1 %while.20 = (s32[]{:T(128)}, f32[16,128,256]{2,1,0:T(8,128)}, s32[]{:T(128)}, s32[128]{0:T(128)S(1)}, bf16[128,128,128]{2,1,0:T(8,128)(2,1)}, /*index=5*/s32[128...) while((s32[]{:T(128)}, f32[16,128,256]{2,1,0:T(8,128)}, ...), condition=%wide.region_2.3_spmd, body=%wide.region_0.2_spmd.sunk | while | flops 67634272 | bytes 6033919 | solution.py:91
  157.3 3.3 scatter_fusion
  163.2 3.3 scatter_fusion
  169.2 3.3 scatter_fusion
  175.1 3.3 scatter_fusion
  181.0 3.3 scatter_fusion
  187.0 3.3 scatter_fusion
  192.9 3.2 scatter_fusion
  198.8 3.3 scatter_fusion
  204.7 3.3 scatter_fusion
  210.6 3.3 scatter_fusion
  216.6 3.3 scatter_fusion
  222.6 3.3 scatter_fusion
  228.5 3.3 scatter_fusion
  231.8 2.7 convert_element_type.37
  234.5 23.4 %all-to-all-start.1 = ((bf16[16,128,256]{2,1,0:T(8,128)(2,1)}), bf16[16,128,256]{2,1,0:T(8,128)(2,1)S(1)}, u32[]{:S(2)}, u32[]{:S(2)}) async-start(bf16[16,128,256]{2,1,0:T(8,128)(2,1)} %convert_element_type.37), calls=%async_computation.1 | async-start | bytes 2097152 | tf_op jit(solution)/shard_map/all_to_all | solution.py:34
  258.3 27.8 %all-to-all-done.1 = bf16[16,128,256]{2,1,0:T(8,128)(2,1)S(1)} async-done(((bf16[16,128,256]{2,1,0:T(8,128)(2,1)}), bf16[16,128,256]{2,1,0:T(8,128)(2,1)S(1)}, u32[]{:S(2)}, u32[]{:S(2)}) %all-to-all-start.1) | async-done | bytes 1048608 | tf_op jit(solution)/shard_map/all_to_all | solution.py:34
  289.0 269.7 %all-reduce.2.cloned.1.call-done = f32[256,256]{0,1:T(8,128)} async-done(((f32[256,256]{0,1:T(8,128)}), f32[256,256]{0,1:T(8,128)}) %all-reduce.2.cloned.1.call-update) | async-done | bytes 262160 | tf_op jit(solution)/shard_map/psum | solution.py:158
  (174 shorter events, 111.9 us)
Async XLA Ops:
  7.2 280.2 %copy-start = (bf16[256,256]{1,0:T(8,128)(2,1)S(1)}, bf16[256,256]{1,0:T(8,128)(2,1)}, u32[]{:S(2)}) copy-start(bf16[256,256]{1,0:T(8,128)(2,1)} %param.16) | copy-start | bytes 393220
  9.2 37.4 %all-to-all-start.2 = ((bf16[16,1,128,256]{3,2,1,0:T(8,128)(2,1)}), bf16[16,1,128,256]{3,2,1,0:T(8,128)(2,1)}, u32[]{:S(2)}, u32[]{:S(2)}) async-start(bf16[16,1,128,256]{3,2,1,0:T(8,128)(2,1)} %broadcast_in_dim.43), calls=%async_computation.2 | async-start | bytes 2097152 | tf_op jit(solution)/shard_map/all_to_all | solution.py:12
  18.4 28.2 %copy-start.5 = (bf16[1,32,256]{2,1,0:T(8,128)(2,1)S(1)}, bf16[1,32,256]{2,1,0:T(8,128)(2,1)}, u32[]{:S(2)}) copy-start(bf16[1,32,256]{2,1,0:T(8,128)(2,1)} %param.18) | copy-start | bytes 49156
  24.7 35.2 %copy-start.2 = (s32[1,128]{1,0:T(1,128)S(1)}, s32[1,128]{1,0:T(1,128)}, u32[]{:S(2)}) copy-start(s32[1,128]{1,0:T(1,128)} %param.20) | copy-start | bytes 1540
  24.8 35.2 %copy-start.3 = (s32[1,128]{1,0:T(1,128)S(1)}, s32[1,128]{1,0:T(1,128)}, u32[]{:S(2)}) copy-start(s32[1,128]{1,0:T(1,128)} %param.21) | copy-start | bytes 1540
  24.8 35.2 %copy-start.4 = (s32[1,128]{1,0:T(1,128)S(1)}, s32[1,128]{1,0:T(1,128)}, u32[]{:S(2)}) copy-start(s32[1,128]{1,0:T(1,128)} %param.22) | copy-start | bytes 1540
  47.4 81.4 %all-to-all-start = ((bf16[32,1,32,256]{3,2,1,0:T(8,128)(2,1)}), bf16[32,1,32,256]{3,2,1,0:T(8,128)(2,1)S(1)}, u32[]{:S(2)}, u32[]{:S(2)}) async-start(bf16[32,1,32,256]{3,2,1,0:T(8,128)(2,1)} %broadcast_in_dim.40), calls=%async_computation | async-start | bytes 1048576 | tf_op jit(solution)/shard_map/all_to_all | solution.py:12
  128.8 105.7 %all-to-all-start.3 = ((bf16[32,32,256]{2,1,0:T(8,128)(2,1)}), bf16[32,32,256]{2,1,0:T(8,128)(2,1)S(1)}, u32[]{:S(2)}, u32[]{:S(2)}) async-start(bf16[32,32,256]{2,1,0:T(8,128)(2,1)} %bitcast.11), calls=%async_computation.3 | async-start | bytes 1048576 | tf_op jit(solution)/shard_map/all_to_all | solution.py:34
  234.5 23.5 %copy-start.6 = (bf16[1,32,256]{2,1,0:T(8,128)(2,1)S(1)}, bf16[1,32,256]{2,1,0:T(8,128)(2,1)}, u32[]{:S(2)}) copy-start(bf16[1,32,256]{2,1,0:T(8,128)(2,1)} %param.15) | copy-start | bytes 49156
  234.5 51.8 %copy-start.1 = (bf16[1,128,256]{2,1,0:T(8,128)(2,1)S(1)}, bf16[1,128,256]{2,1,0:T(8,128)(2,1)}, u32[]{:S(2)}) copy-start(bf16[1,128,256]{2,1,0:T(8,128)(2,1)} %param.14) | copy-start | bytes 196612
  234.5 51.7 %all-to-all-start.1 = ((bf16[16,128,256]{2,1,0:T(8,128)(2,1)}), bf16[16,128,256]{2,1,0:T(8,128)(2,1)S(1)}, u32[]{:S(2)}, u32[]{:S(2)}) async-start(bf16[16,128,256]{2,1,0:T(8,128)(2,1)} %convert_element_type.37), calls=%async_computation.1 | async-start | bytes 2097152 | tf_op jit(solution)/shard_map/all_to_all | solution.py:34
  257.9 300.8 %all-reduce.2.cloned.1.call-start = ((), (), s32[]{:S(2)}) async-start(), calls=%async_computation.4 | async-start | bytes 524288 | tf_op jit(solution)/shard_map/psum | solution.py:158
Sparse Core Ops, SparseCore 0:
  287.5 271.1 all-reduce.1
where the time goes:
time: 570 us; the launch traced here: 567 us
  waiting for transfers between devices  319 us (56%)
  other arithmetic  85.7 us (15%)
  starting transfers between devices  68.7 us (12%)
  local copies, waits for them, and re-layouts  42.9 us (8%)
  matrix products  35.1 us (6%)
  between operations  14.8 us (3%)
    psum x1, waiting for transfers between devices, per_device(): lax.psum(weight_part, ('au', 'ia')) / math.sqrt(user_count + item_count)  270 us
    all_to_all x2, starting transfers between devices, summed_on_arrival(): lax.all_to_all(pieces, axis, split_axis=0, concat_axis=0, tiled=True)  47.7 us
    scatter-add x13, other arithmetic, one_turn(): user_total = user_total.at[row_pick].add(forward * inverse)  42.8 us
    all_to_all x2, waiting for transfers between devices, summed_on_arrival(): lax.all_to_all(pieces, axis, split_axis=0, concat_axis=0, tiled=True)  27.8 us
    gather x13, local copies, waits for them, and re-layouts, one_turn(): user_source[row_pick]  23.5 us
    all_to_all x2, waiting for transfers between devices, from_everyone(): return lax.all_to_all(copies, axis, split_axis=0, concat_axis=0, tiled=True)  21.8 us
    all_to_all x2, starting transfers between devices, from_everyone(): return lax.all_to_all(copies, axis, split_axis=0, concat_axis=0, tiled=True)  20.9 us
    select_n x26, other arithmetic, one_turn(): jnp.where(live_mask, 1.0 / norm_pick.astype(jnp.float32), 0.0)  18.8 us
  transfers between devices with their start and end apart: 5, of which 3 were waited for; matrix products, arithmetic and copies ran while one was open for 28% of the time, Pallas kernels for 0%

commit v1 on v0

--- a/solution.py
+++ b/solution.py
@@ -155,7 +155,7 @@
     weight_part = block_product(user_emb[0], q_user) + block_product(item_emb[0], q_item)
     user_count = user_emb.shape[1] * lax.axis_size("ia") * lax.axis_size("au")
     item_count = item_emb.shape[1] * lax.axis_size("au") * lax.axis_size("ia")
-    grad_weight = lax.psum(weight_part, ("au", "ia")) / math.sqrt(user_count + item_count)
+    grad_weight = lax.psum(lax.psum(weight_part, "au"), "ia") / math.sqrt(user_count + item_count)
     grad_user_emb = jnp.einsum(
         "re,de->rd", q_user.astype(jnp.bfloat16), weight, preferred_element_type=jnp.float32
     ).astype(jnp.bfloat16)

time: 570 us -> 795 us (1.39)
  the two profiles are of different devices: /device:TPU:23 before, /device:TPU:1 now
where the time goes in v1:
time: 795 us; the launch traced here: 792 us
  waiting for transfers between devices  541 us (68%)
  starting transfers between devices  94.3 us (12%)
  other arithmetic  73.2 us (9%)
  local copies, waits for them, and re-layouts  38.1 us (5%)
  matrix products  30.2 us (4%)
  between operations  14.8 us (2%)
    psum x1, waiting for transfers between devices, per_device(): lax.psum(weight_part, 'au')  298 us
    psum x1, waiting for transfers between devices, per_device(): lax.psum(lax.psum(weight_part, 'au'), 'ia')  206 us
    all_to_all x2, starting transfers between devices, summed_on_arrival(): lax.all_to_all(pieces, axis, split_axis=0, concat_axis=0, tiled=True)  66.9 us
    scatter-add x11, other arithmetic, one_turn(): user_total = user_total.at[row_pick].add(forward * inverse)  36.1 us
    all_to_all x2, starting transfers between devices, from_everyone(): return lax.all_to_all(copies, axis, split_axis=0, concat_axis=0, tiled=True)  27.3 us
    gather x11, local copies, waits for them, and re-layouts, one_turn(): user_source[row_pick]  19.9 us
    all_to_all x2, waiting for transfers between devices, summed_on_arrival(): lax.all_to_all(pieces, axis, split_axis=0, concat_axis=0, tiled=True)  19.3 us
    all_to_all x2, waiting for transfers between devices, from_everyone(): return lax.all_to_all(copies, axis, split_axis=0, concat_axis=0, tiled=True)  18.3 us
  transfers between devices with their start and end apart: 6, of which 4 were waited for; matrix products, arithmetic and copies ran while one was open for 17% of the time, Pallas kernels for 0%

profile of v1, /device:TPU:1, one launch (start us, length us, event | category | flops | bytes accessed | tf_op | source)
XLA Modules:
  0.0 792.2 jit_solution(12761285709459915911)
XLA Ops:
  7.2 2.0 broadcast_in_dim.43
  9.2 11.1 %all-to-all-start.2 = ((bf16[16,1,128,256]{3,2,1,0:T(8,128)(2,1)}), bf16[16,1,128,256]{3,2,1,0:T(8,128)(2,1)}, u32[]{:S(2)}, u32[]{:S(2)}) async-start(bf16[16,1,128,256]{3,2,1,0:T(8,128)(2,1)} %broadcast_in_dim.43), calls=%async_computation.2 | async-start | bytes 2097152 | tf_op jit(solution)/shard_map/all_to_all | solution.py:12
  20.9 6.4 copy.16
  27.3 18.3 %all-to-all-done.2 = bf16[16,1,128,256]{3,2,1,0:T(8,128)(2,1)} async-done(((bf16[16,1,128,256]{3,2,1,0:T(8,128)(2,1)}), bf16[16,1,128,256]{3,2,1,0:T(8,128)(2,1)}, u32[]{:S(2)}, u32[]{:S(2)}) %all-to-all-start.2) | async-done | bytes 1048608 | tf_op jit(solution)/shard_map/all_to_all | solution.py:12
  46.4 16.3 %all-to-all-start = ((bf16[32,1,32,256]{3,2,1,0:T(8,128)(2,1)}), bf16[32,1,32,256]{3,2,1,0:T(8,128)(2,1)S(1)}, u32[]{:S(2)}, u32[]{:S(2)}) async-start(bf16[32,1,32,256]{3,2,1,0:T(8,128)(2,1)} %broadcast_in_dim.40), calls=%async_computation | async-start | bytes 1048576 | tf_op jit(solution)/shard_map/all_to_all | solution.py:12
  62.8 57.5 %while.21 = (s32[]{:T(128)}, f32[8,128,256]{2,1,0:T(8,128)S(1)}, s32[]{:T(128)}, s32[128]{0:T(128)S(1)}, bf16[128,128,128]{1,2,0:T(8,128)(2,1)}, /*index=5*/s32[...) while((s32[]{:T(128)}, f32[8,128,256]{2,1,0:T(8,128)S(1)}, ...), condition=%wide.region_6.7_spmd, body=%wide.region_4.6_spmd.sunk | while | flops 67634272 | bytes 6033919 | solution.py:91
  121.2 34.8 %all-to-all-start.3 = ((bf16[32,32,256]{2,1,0:T(8,128)(2,1)}), bf16[32,32,256]{2,1,0:T(8,128)(2,1)S(1)}, u32[]{:S(2)}, u32[]{:S(2)}) async-start(bf16[32,32,256]{2,1,0:T(8,128)(2,1)} %bitcast.11), calls=%async_computation.3 | async-start | bytes 1048576 | tf_op jit(solution)/shard_map/all_to_all | solution.py:34
  157.6 65.2 %while.20 = (s32[]{:T(128)}, f32[16,128,256]{2,1,0:T(8,128)}, s32[]{:T(128)}, s32[128]{0:T(128)S(1)}, bf16[128,128,128]{2,1,0:T(8,128)(2,1)}, /*index=5*/s32[128...) while((s32[]{:T(128)}, f32[16,128,256]{2,1,0:T(8,128)}, ...), condition=%wide.region_2.3_spmd, body=%wide.region_0.2_spmd.sunk | while | flops 67634272 | bytes 6033919 | solution.py:91
  160.3 3.3 scatter_fusion
  166.2 3.3 scatter_fusion
  172.2 3.3 scatter_fusion
  178.1 3.3 scatter_fusion
  184.0 3.3 scatter_fusion
  190.0 3.3 scatter_fusion
  195.9 3.3 scatter_fusion
  201.8 3.2 scatter_fusion
  207.7 3.3 scatter_fusion
  213.7 3.2 scatter_fusion
  219.6 3.3 scatter_fusion
  222.8 2.7 convert_element_type.37
  225.6 32.0 %all-to-all-start.1 = ((bf16[16,128,256]{2,1,0:T(8,128)(2,1)}), bf16[16,128,256]{2,1,0:T(8,128)(2,1)S(1)}, u32[]{:S(2)}, u32[]{:S(2)}) async-start(bf16[16,128,256]{2,1,0:T(8,128)(2,1)} %convert_element_type.37), calls=%async_computation.1 | async-start | bytes 2097152 | tf_op jit(solution)/shard_map/all_to_all | solution.py:34
  258.0 19.2 %all-to-all-done.1 = bf16[16,128,256]{2,1,0:T(8,128)(2,1)S(1)} async-done(((bf16[16,128,256]{2,1,0:T(8,128)(2,1)}), bf16[16,128,256]{2,1,0:T(8,128)(2,1)S(1)}, u32[]{:S(2)}, u32[]{:S(2)}) %all-to-all-start.1) | async-done | bytes 1048608 | tf_op jit(solution)/shard_map/all_to_all | solution.py:34
  278.5 297.7 %all-reduce.3.cloned.1.call-done = f32[256,256]{0,1:T(8,128)} async-done(((f32[256,256]{0,1:T(8,128)}), f32[256,256]{0,1:T(8,128)}) %all-reduce.3.cloned.1.call-update) | async-done | bytes 262160 | tf_op jit(solution)/shard_map/psum | solution.py:158
  577.9 205.6 %all-reduce.5.cloned.1.call-done = f32[256,256]{0,1:T(8,128)} async-done(((f32[256,256]{0,1:T(8,128)}), f32[256,256]{0,1:T(8,128)}) %all-reduce.5.cloned.1.call-update) | async-done | bytes 262160 | tf_op jit(solution)/shard_map/psum | solution.py:158
  (153 shorter events, 94.4 us)
Async XLA Ops:
  7.2 569.1 %copy-start = (bf16[256,256]{1,0:T(8,128)(2,1)S(1)}, bf16[256,256]{1,0:T(8,128)(2,1)}, u32[]{:S(2)}) copy-start(bf16[256,256]{1,0:T(8,128)(2,1)} %param.16) | copy-start | bytes 393220
  9.2 36.4 %all-to-all-start.2 = ((bf16[16,1,128,256]{3,2,1,0:T(8,128)(2,1)}), bf16[16,1,128,256]{3,2,1,0:T(8,128)(2,1)}, u32[]{:S(2)}, u32[]{:S(2)}) async-start(bf16[16,1,128,256]{3,2,1,0:T(8,128)(2,1)} %broadcast_in_dim.43), calls=%async_computation.2 | async-start | bytes 2097152 | tf_op jit(solution)/shard_map/all_to_all | solution.py:12
  20.9 24.7 %copy-start.5 = (bf16[1,32,256]{2,1,0:T(8,128)(2,1)S(1)}, bf16[1,32,256]{2,1,0:T(8,128)(2,1)}, u32[]{:S(2)}) copy-start(bf16[1,32,256]{2,1,0:T(8,128)(2,1)} %param.18) | copy-start | bytes 49156
  27.3 35.5 %copy-start.2 = (s32[1,128]{1,0:T(1,128)S(1)}, s32[1,128]{1,0:T(1,128)}, u32[]{:S(2)}) copy-start(s32[1,128]{1,0:T(1,128)} %param.20) | copy-start | bytes 1540
  27.3 35.6 %copy-start.3 = (s32[1,128]{1,0:T(1,128)S(1)}, s32[1,128]{1,0:T(1,128)}, u32[]{:S(2)}) copy-start(s32[1,128]{1,0:T(1,128)} %param.21) | copy-start | bytes 1540
  27.3 35.6 %copy-start.4 = (s32[1,128]{1,0:T(1,128)S(1)}, s32[1,128]{1,0:T(1,128)}, u32[]{:S(2)}) copy-start(s32[1,128]{1,0:T(1,128)} %param.22) | copy-start | bytes 1540
  46.4 74.8 %all-to-all-start = ((bf16[32,1,32,256]{3,2,1,0:T(8,128)(2,1)}), bf16[32,1,32,256]{3,2,1,0:T(8,128)(2,1)S(1)}, u32[]{:S(2)}, u32[]{:S(2)}) async-start(bf16[32,1,32,256]{3,2,1,0:T(8,128)(2,1)} %broadcast_in_dim.40), calls=%async_computation | async-start | bytes 1048576 | tf_op jit(solution)/shard_map/all_to_all | solution.py:12
  121.2 104.3 %all-to-all-start.3 = ((bf16[32,32,256]{2,1,0:T(8,128)(2,1)}), bf16[32,32,256]{2,1,0:T(8,128)(2,1)S(1)}, u32[]{:S(2)}, u32[]{:S(2)}) async-start(bf16[32,32,256]{2,1,0:T(8,128)(2,1)} %bitcast.11), calls=%async_computation.3 | async-start | bytes 1048576 | tf_op jit(solution)/shard_map/all_to_all | solution.py:34
  225.5 32.2 %copy-start.6 = (bf16[1,32,256]{2,1,0:T(8,128)(2,1)S(1)}, bf16[1,32,256]{2,1,0:T(8,128)(2,1)}, u32[]{:S(2)}) copy-start(bf16[1,32,256]{2,1,0:T(8,128)(2,1)} %param.15) | copy-start | bytes 49156
  225.5 51.9 %copy-start.1 = (bf16[1,128,256]{2,1,0:T(8,128)(2,1)S(1)}, bf16[1,128,256]{2,1,0:T(8,128)(2,1)}, u32[]{:S(2)}) copy-start(bf16[1,128,256]{2,1,0:T(8,128)(2,1)} %param.14) | copy-start | bytes 196612
  225.6 51.7 %all-to-all-start.1 = ((bf16[16,128,256]{2,1,0:T(8,128)(2,1)}), bf16[16,128,256]{2,1,0:T(8,128)(2,1)S(1)}, u32[]{:S(2)}, u32[]{:S(2)}) async-start(bf16[16,128,256]{2,1,0:T(8,128)(2,1)} %convert_element_type.37), calls=%async_computation.1 | async-start | bytes 2097152 | tf_op jit(solution)/shard_map/all_to_all | solution.py:34
  257.6 318.7 %all-reduce.3.cloned.1.call-start = ((), (), s32[]{:S(2)}) async-start(), calls=%async_computation.4 | async-start | bytes 524288 | tf_op jit(solution)/shard_map/psum | solution.py:158
  278.5 505.1 %all-reduce.5.cloned.1.call-start = ((), (), s32[]{:S(2)}) async-start(), calls=%async_computation.5 | async-start | bytes 524288 | tf_op jit(solution)/shard_map/psum | solution.py:158
Sparse Core Ops, SparseCore 0:
  278.6 297.6 all-reduce.2
  579.2 204.3 all-reduce.4
